TPU v7x, 256 devices: a whole 4x4x8 slice. The times are simulated.
256 devices in a mesh: context: 32 (over x, z), mirror: 2 (over core), tensor: 4 (over y).
Axes of the slice: x: 4, y: 4, z: 8, core: 2. Of those that a mesh axis runs over, the one named last changes fastest.
Arguments:
- hyena_q: bfloat16 [8192, 8192], P(('context', 'mirror'), 'tensor'), may hold values from -57 to 57
- hyena_k: bfloat16 [8192, 8192], P(('context', 'mirror'), 'tensor'), may hold values from -6 to 6
- hyena_v: bfloat16 [8192, 8192], P(('context', 'mirror'), 'tensor'), may hold values from -6 to 6
- filters: bfloat16 [512, 128], P('tensor'), may hold values from -0.5 to 0.5
- norm_gain: float32 [8192], P('tensor'), may hold values from 0.1 to 1.9
- attn_q: bfloat16 [8192, 8192], P(('context', 'mirror'), 'tensor'), may hold values from -35 to 35
- attn_k: bfloat16 [8192, 8192], P(('context', 'mirror'), 'tensor'), may hold values from -5 to 5
- out_grad: bfloat16 [8192, 8192], P(('context', 'mirror'), 'tensor'), may hold values from -20 to 20
- doc_lengths: int32 [4], replicated, may hold values from 1 to 4096, 8192 in all
Outputs:
- attn_out: bfloat16 [8192, 8192], P(('context', 'mirror'), 'tensor')
- grad_attn_q: bfloat16 [8192, 8192], P(('context', 'mirror'), 'tensor')
- grad_attn_k: bfloat16 [8192, 8192], P(('context', 'mirror'), 'tensor')
- grad_hyena_q: bfloat16 [8192, 8192], P(('context', 'mirror'), 'tensor')
- grad_hyena_k: bfloat16 [8192, 8192], P(('context', 'mirror'), 'tensor')
- grad_hyena_v: bfloat16 [8192, 8192], P(('context', 'mirror'), 'tensor')
- grad_filters: float32 [512, 128], P('tensor')
All inputs are finite; a program needn't handle non-finite values.
Results may differ from a plain program's by a relative error of at most 0.0064.
Values may be sent and summed in bfloat16 or wider, within the bound.
No kernel may reach another device: no remote copies, remote signals or barrier semaphores. Data moves between devices by JAX's collectives and lax.ppermute only.
A program may use at most 128 MiB of HBM per device.

v0:
```python
import jax
import jax.numpy as jnp
from jax import lax
from jax.sharding import PartitionSpec as P

HEAD = 128
D = 8192
REACH = 2


def passed_along(block, axis, distance):
    devices = range(lax.axis_size(axis))
    route = [(i - distance, i) for i in devices if i - distance in devices]
    return lax.ppermute(block, axis, route)


def doc_index(doc_lengths, positions):
    doc_ends = jnp.cumsum(doc_lengths, dtype=jnp.int32)
    return jnp.sum(
        (positions[:, None] >= doc_ends[None, :]).astype(jnp.int32), axis=1, dtype=jnp.int32
    )


def banded(band_table, row_count, col_count):
    repeated = jnp.tile(band_table, (1, row_count + 1))[:, : row_count * col_count]
    return repeated.reshape(band_table.shape[0], row_count, col_count)


def attend(queries, key_heads, allowed, score_scale):
    scores = (
        jnp.einsum("thd,uhd->htu", queries, key_heads, preferred_element_type=jnp.float32)
        * score_scale
    )
    row_top = jnp.max(jnp.where(allowed[None], scores, -1e30), axis=2, keepdims=True)
    row_total = jnp.sum(
        jnp.exp(jnp.where(allowed[None], scores - row_top, -1e30)), axis=2, keepdims=True
    )
    row_lse = row_top + jnp.log(row_total)
    return (jnp.where(allowed[None], jnp.exp(scores - row_lse), 0.0), row_lse)


def body(hyena_q, hyena_k, hyena_v, filters, norm_gain, attn_q, attn_k, out_grad, doc_lengths):
    tok_rows, channels = hyena_q.shape
    groups, tap_count = filters.shape
    group_width = channels // groups
    heads_dev = channels // HEAD
    pad_rows = tok_rows + tap_count
    offset = lax.axis_index(("context", "mirror")) * tok_rows
    score_scale = HEAD ** (-0.5)
    window_span = REACH * tok_rows
    own_pos = offset + jnp.arange(tok_rows, dtype=jnp.int32)
    own_doc = doc_index(doc_lengths, own_pos)
    kv_product = (hyena_k.astype(jnp.float32) * hyena_v.astype(jnp.float32)).astype(jnp.bfloat16)
    left_rim = passed_along(kv_product[tok_rows - (tap_count - 1) :], ("context", "mirror"), 1)
    wide_pad = jnp.concatenate(
        [left_rim, kv_product, jnp.zeros((1, channels), jnp.bfloat16)], axis=0
    )
    wide_pos = offset - (tap_count - 1) + jnp.arange(pad_rows, dtype=jnp.int32)
    fwd_mask = own_doc[:, None] == doc_index(doc_lengths, wide_pos)[None, :]
    zeros_tail = jnp.zeros((groups, pad_rows + 1 - tap_count), jnp.bfloat16)
    fwd_table = jnp.concatenate([filters[:, ::-1], zeros_tail], axis=1)
    fwd_band = banded(fwd_table, tok_rows, pad_rows) * fwd_mask[None].astype(jnp.bfloat16)
    wide_groups = wide_pad.reshape(pad_rows, groups, group_width)
    signal = jnp.einsum(
        "gtu,ugc->tgc", fwd_band, wide_groups, preferred_element_type=jnp.float32
    ).reshape(tok_rows, channels)
    hyena_mix = hyena_q.astype(jnp.float32) * signal
    square_sum = lax.psum(jnp.sum(hyena_mix * hyena_mix, axis=1), "tensor")
    inv_rms = lax.rsqrt(square_sum / D + 1e-06)
    values = (hyena_mix * inv_rms[:, None] * norm_gain[None, :]).astype(jnp.bfloat16)
    earlier = []
    for distance in range(1, REACH + 1):
        earlier.append(passed_along((attn_k, values), ("context", "mirror"), distance))
    key_win = jnp.concatenate([piece[0] for piece in earlier[::-1]] + [attn_k], axis=0)
    value_win = jnp.concatenate([piece[1] for piece in earlier[::-1]] + [values], axis=0)
    window = (REACH + 1) * tok_rows
    key_pos = offset - REACH * tok_rows + jnp.arange(window, dtype=jnp.int32)
    key_doc = doc_index(doc_lengths, key_pos)
    allowed = (
        (key_pos[None, :] >= 0)
        & (key_pos[None, :] <= own_pos[:, None])
        & (own_pos[:, None] - key_pos[None, :] <= window_span)
        & (key_doc[None, :] == own_doc[:, None])
    )
    queries = attn_q.reshape(tok_rows, heads_dev, HEAD)
    grad_heads = out_grad.reshape(tok_rows, heads_dev, HEAD)
    key_heads = key_win.reshape(window, heads_dev, HEAD)
    value_heads = value_win.reshape(window, heads_dev, HEAD)
    attn_prob, row_lse = attend(queries, key_heads, allowed, score_scale)
    prob_half = attn_prob.astype(jnp.bfloat16)
    attn_out = (
        jnp.einsum("htu,uhd->thd", prob_half, value_heads, preferred_element_type=jnp.float32)
        .astype(jnp.bfloat16)
        .reshape(tok_rows, channels)
    )
    grad_prob = jnp.einsum(
        "thd,uhd->htu", grad_heads, value_heads, preferred_element_type=jnp.float32
    )
    row_delta = jnp.sum(attn_prob * grad_prob, axis=2, keepdims=True)
    grad_score = (attn_prob * (grad_prob - row_delta) * score_scale).astype(jnp.bfloat16)
    grad_attn_q = (
        jnp.einsum("htu,uhd->thd", grad_score, key_heads, preferred_element_type=jnp.float32)
        .astype(jnp.bfloat16)
        .reshape(tok_rows, channels)
    )
    own_start = REACH * tok_rows
    key_part = jnp.einsum("htu,thd->uhd", grad_score, queries, preferred_element_type=jnp.float32)
    value_part = jnp.einsum(
        "htu,thd->uhd", prob_half, grad_heads, preferred_element_type=jnp.float32
    )
    grad_keys = key_part[own_start:]
    grad_vals = value_part[own_start:]
    for distance in range(1, REACH + 1):
        low_row = (REACH - distance) * tok_rows
        returned = passed_along(
            (key_part[low_row : low_row + tok_rows], value_part[low_row : low_row + tok_rows]),
            ("context", "mirror"),
            -distance,
        )
        grad_keys = grad_keys + returned[0]
        grad_vals = grad_vals + returned[1]
    grad_attn_k = grad_keys.astype(jnp.bfloat16).reshape(tok_rows, channels)
    grad_values = grad_vals.reshape(tok_rows, channels)
    inner_sum = lax.psum(jnp.sum(norm_gain[None, :] * grad_values * hyena_mix, axis=1), "tensor")
    grad_mix = inv_rms[:, None] * (
        norm_gain[None, :] * grad_values - hyena_mix * (inner_sum * inv_rms * inv_rms / D)[:, None]
    )
    grad_hyena_q = (grad_mix * signal).astype(jnp.bfloat16)
    grad_signal = (grad_mix * hyena_q.astype(jnp.float32)).astype(jnp.bfloat16)
    right_rim = passed_along(grad_signal[: tap_count - 1], ("context", "mirror"), -1)
    back_pad = jnp.concatenate(
        [grad_signal, right_rim, jnp.zeros((1, channels), jnp.bfloat16)], axis=0
    )
    back_pos = offset + jnp.arange(pad_rows, dtype=jnp.int32)
    back_mask = own_doc[:, None] == doc_index(doc_lengths, back_pos)[None, :]
    back_table = jnp.concatenate([filters, zeros_tail], axis=1)
    back_band = banded(back_table, tok_rows, pad_rows) * back_mask[None].astype(jnp.bfloat16)
    grad_kv = jnp.einsum(
        "gtu,ugc->tgc",
        back_band,
        back_pad.reshape(pad_rows, groups, group_width),
        preferred_element_type=jnp.float32,
    ).reshape(tok_rows, channels)
    grad_hyena_k = (grad_kv * hyena_v.astype(jnp.float32)).astype(jnp.bfloat16)
    grad_hyena_v = (grad_kv * hyena_k.astype(jnp.float32)).astype(jnp.bfloat16)
    block_count = 4
    block_size = groups // block_count
    mask_float = fwd_mask.astype(jnp.float32)

    def filter_block(pieces):
        grad_block, wide_block = pieces
        correlation = (
            jnp.einsum("tgc,ugc->gtu", grad_block, wide_block, preferred_element_type=jnp.float32)
            * mask_float[None]
        )
        flattened = jnp.pad(
            correlation.reshape(block_size, tok_rows * pad_rows), ((0, 0), (0, tok_rows))
        )
        diagonal = flattened.reshape(block_size, tok_rows, pad_rows + 1)[:, :, :tap_count]
        return jnp.sum(diagonal, axis=1)[:, ::-1]

    grad_blocks = grad_signal.reshape(tok_rows, block_count, block_size, group_width).transpose(
        1, 0, 2, 3
    )
    wide_blocks = wide_groups.reshape(pad_rows, block_count, block_size, group_width).transpose(
        1, 0, 2, 3
    )
    local_filters = lax.map(filter_block, (grad_blocks, wide_blocks)).reshape(groups, tap_count)
    grad_filters = lax.psum(local_filters, ("context", "mirror"))
    return (
        attn_out,
        grad_attn_q,
        grad_attn_k,
        grad_hyena_q,
        grad_hyena_k,
        grad_hyena_v,
        grad_filters,
    )


def solution(mesh):
    return jax.shard_map(
        body,
        mesh=mesh,
        in_specs=(
            P(("context", "mirror"), "tensor"),
            P(("context", "mirror"), "tensor"),
            P(("context", "mirror"), "tensor"),
            P("tensor", None),
            P("tensor"),
            P(("context", "mirror"), "tensor"),
            P(("context", "mirror"), "tensor"),
            P(("context", "mirror"), "tensor"),
            P(),
        ),
        out_specs=(
            P(("context", "mirror"), "tensor"),
            P(("context", "mirror"), "tensor"),
            P(("context", "mirror"), "tensor"),
            P(("context", "mirror"), "tensor"),
            P(("context", "mirror"), "tensor"),
            P(("context", "mirror"), "tensor"),
            P("tensor", None),
        ),
        check_vma=False,
    )
```

profile of v0, /device:TPU:1, one launch (start us, length us, event | category | flops | bytes accessed | tf_op | source)
XLA Modules:
  0.0 418.3 jit_solution(6076285192775258305)
XLA Ops:
  8.6 5.1 %collective-permute-start.4 = (bf16[128,2048]{0,1:T(8,128)(2,1)S(1)}, bf16[128,2048]{0,1:T(8,128)(2,1)}, u32[]{:S(2)}, u32[]{:S(2)}) collective-permute-start(bf16[128,2048]{0,1:T(8,128)(2,1)S(1)} %copy.70), channel_id=1, source_target_pairs={{0,4},{4,8},{8,12},{12,16},{16,20},{20,24},{24,28},{28,32},{32,36}... | collective-permute-start | bytes 1572872 | tf_op jit(solution)/shard_map/ppermute | solution.py:14
  13.7 4.4 %collective-permute-start.3 = (bf16[128,2048]{0,1:T(8,128)(2,1)S(1)}, bf16[128,2048]{0,1:T(8,128)(2,1)}, u32[]{:S(2)}, u32[]{:S(2)}) collective-permute-start(bf16[128,2048]{0,1:T(8,128)(2,1)S(1)} %copy.70), channel_id=1, source_target_pairs={{0,8},{4,12},{8,16},{12,20},{16,24},{20,28},{24,32},{28,36},{32,40... | collective-permute-start | bytes 1572872 | tf_op jit(solution)/shard_map/ppermute | solution.py:14
  28.5 4.5 %tile.8 = bf16[128,129,257]{0,2,1:T(8,128)(2,1)} broadcast(bf16[128,257]{0,1:T(8,128)(2,1)S(1)} %concatenate.19.clone), dimensions={0,2} | broadcast | bytes 8552960 | tf_op jit(solution)/shard_map/tile | solution.py:25
  33.0 13.2 %tile.9 = bf16[128,33153]{0,1:T(8,128)(2,1)} reshape(bf16[128,129,257]{0,2,1:T(8,128)(2,1)} %tile.8) | data formatting | bytes 16974336 | tf_op jit(solution)/shard_map/tile | solution.py:25
  46.3 7.1 %slice.49 = bf16[128,32768]{0,1:T(8,128)(2,1)} slice(bf16[128,33153]{0,1:T(8,128)(2,1)} %tile.9), slice={[0:128], [0:32768]} | slice | bytes 16777216 | tf_op jit(solution)/shard_map/slice | solution.py:25
  53.3 12.5 %copy.69 = bf16[128,128,256]{2,1,0:T(8,128)(2,1)} copy(bf16[128,128,256]{0,2,1:T(8,128)(2,1)} %bitcast.165) | data formatting | bytes 16777216 | tf_op jit(solution)/shard_map/reshape | solution.py:26
  65.8 4.5 %tile.20 = bf16[128,129,257]{0,2,1:T(8,128)(2,1)} broadcast(bf16[128,257]{0,1:T(8,128)(2,1)S(1)} %concatenate.23.clone), dimensions={0,2} | broadcast | bytes 8552960 | tf_op jit(solution)/shard_map/tile | solution.py:25
  70.3 13.2 %tile.21 = bf16[128,33153]{0,1:T(8,128)(2,1)} reshape(bf16[128,129,257]{0,2,1:T(8,128)(2,1)} %tile.20) | data formatting | bytes 16974336 | tf_op jit(solution)/shard_map/tile | solution.py:25
  83.5 7.1 %slice.57 = bf16[128,32768]{0,1:T(8,128)(2,1)} slice(bf16[128,33153]{0,1:T(8,128)(2,1)} %tile.21), slice={[0:128], [0:32768]} | slice | bytes 16777216 | tf_op jit(solution)/shard_map/slice | solution.py:25
  90.6 12.6 %copy.84 = bf16[128,128,256]{2,1,0:T(8,128)(2,1)} copy(bf16[128,128,256]{0,2,1:T(8,128)(2,1)} %bitcast.166) | data formatting | bytes 16777216 | tf_op jit(solution)/shard_map/reshape | solution.py:26
  109.3 3.4 collective-permute-start.7
  116.6 16.7 %collective-permute-done.8 = f32[128,16,128]{0,2,1:T(8,128)S(1)} collective-permute-done((f32[128,16,128]{0,2,1:T(8,128)S(1)}, f32[128,16,128]{0,2,1:T(8,128)S(1)}, u32[]{:S(2)}, u32[]{:S(2)}) %collective-permute-start.8) | collective-permute-done | bytes 1048608 | tf_op jit(solution)/shard_map/ppermute | solution.py:14
  133.3 12.7 %collective-permute-done.7 = f32[128,16,128]{0,2,1:T(8,128)S(1)} collective-permute-done((f32[128,16,128]{0,2,1:T(8,128)S(1)}, f32[128,16,128]{0,2,1:T(8,128)S(1)}, u32[]{:S(2)}, u32[]{:S(2)}) %collective-permute-start.7) | collective-permute-done | bytes 1048608 | tf_op jit(solution)/shard_map/ppermute | solution.py:14
  147.2 8.7 %all-reduce.3 = (f32[128]{0:T(128)S(1)}, f32[128]{0:T(128)S(1)}) all-reduce(f32[128]{0:T(128)S(1)} %get-tuple-element.111, f32[128]{0:T(128)S(1)} %get-tuple-element.110), channel_id=1, replica_groups=mesh['context'=32,'mirror'=2,'tensor'=4] {'tensor'}, use_global_device_ids=true, to_apply=%region_4.5 | all-reduce | flops 256 | bytes 2048 | tf_op jit(solution)/shard_map/psum | solution.py:68
  155.9 3.4 fusion.45
  159.2 3.8 collective-permute-start.2
  163.0 5.2 %collective-permute-start.1 = (bf16[128,2048]{0,1:T(8,128)(2,1)}, bf16[128,2048]{0,1:T(8,128)(2,1)}, u32[]{:S(2)}, u32[]{:S(2)}) collective-permute-start(bf16[128,2048]{0,1:T(8,128)(2,1)} %get-tuple-element.134), channel_id=1, source_target_pairs={{0,8},{4,12},{8,16},{12,20},{16,24},{20,28},{24,32},{28,36},{32,40... | collective-permute-start | bytes 1572872 | tf_op jit(solution)/shard_map/ppermute | solution.py:14
  170.1 67.7 %while.13 = (s32[]{:T(128)}, f32[4,32,128]{2,1,0:T(8,128)}, bf16[4,128,32,16]{1,3,2,0:T(8,128)(2,1)}, bf16[4,256,32,16]{1,3,2,0:T(8,128)(2,1)}, s32[256]{0:T(256...) while((s32[]{:T(128)}, f32[4,32,128]{2,1,0:T(8,128)}, bf16[4,128,32,16]{1,3,2,0:T(8,128)(2,1)}, ...), condition=%wide.region_14.15_spmd.clone, body=%wide.region_12.14_spmd.clone.sunk | while | flops 35188736 | bytes 32246372 | solution.py:168
  172.0 2.4 copy.103
  176.7 8.0 %reshape.319 = f32[32,128,257]{2,1,0:T(8,128)} reshape(f32[32,32896]{1,0:T(8,128)} %pad.33) | data formatting | bytes 8421376 | tf_op jit(solution)/shard_map/while/body/eval_jaxpr/reshape | solution.py:159
  188.9 2.4 copy.103
  193.6 8.0 %reshape.319 = f32[32,128,257]{2,1,0:T(8,128)} reshape(f32[32,32896]{1,0:T(8,128)} %pad.33) | data formatting | bytes 8421376 | tf_op jit(solution)/shard_map/while/body/eval_jaxpr/reshape | solution.py:159
  210.6 8.0 %reshape.319 = f32[32,128,257]{2,1,0:T(8,128)} reshape(f32[32,32896]{1,0:T(8,128)} %pad.33) | data formatting | bytes 8421376 | tf_op jit(solution)/shard_map/while/body/eval_jaxpr/reshape | solution.py:159
  227.5 8.0 %reshape.319 = f32[32,128,257]{2,1,0:T(8,128)} reshape(f32[32,32896]{1,0:T(8,128)} %pad.33) | data formatting | bytes 8421376 | tf_op jit(solution)/shard_map/while/body/eval_jaxpr/reshape | solution.py:159
  241.4 6.7 %fusion.8 = f32[128,16,128]{2,1,0:T(8,128)} fusion(bf16[256,128,16]{0,2,1:T(8,128)(2,1)S(1)} %bitcast.175, bf16[128,128,256]{2,1,0:T(8,128)(2,1)} %copy.84, bf16[128,256]{1,0:T(8,128)(2,1)S(1)} %get-tuple-element.137), kind=kOutput, calls=%fused_computation.11 | convolution fusion | flops 138412032 | bytes 10551296 | tf_op jit(solution)/shard_map/gtu,ugc->tgc/dot_general | solution.py:138
  253.2 6.6 %convolution_bitcast_fusion.1 = f32[384,16,128]{0,2,1:T(8,128)} fusion(bf16[128,16,128]{0,2,1:T(8,128)(2,1)} %bitcast.177, f32[16,384,128]{2,1,0:T(8,128)} %fusion.72, f32[16,384,128]{2,1,0:T(8,128)S(1)} %get-tuple-element.142, f32[16,128]{1,0:T(8,128)S(1)} %log_add_fusion, pred[128,384]{0,1:T(8,128)(4,1)S(1)} %fusion.54), kind=kOutput, calls=%fused_computation.32 | convolution fusion | flops 209979776 | bytes 10018816 | tf_op jit(solution)/shard_map/htu,thd->uhd/dot_general | solution.py:107
  259.8 3.4 fusion.70
  271.9 3.0 convolution_convert_fusion
  276.9 6.2 %fusion.44 = bf16[16,128,128]{2,1,0:T(8,128)(2,1)} fusion(bf16[384,16,128]{0,2,1:T(8,128)(2,1)} %bitcast.172, f32[16,384,128]{2,1,0:T(8,128)} %fusion.72, f32[16,384,128]{2,1,0:T(8,128)S(1)} %get-tuple-element.142, f32[16,128]{1,0:T(8,128)S(1)} %log_add_fusion, pred[128,384]{0,1:T(8,128)(4,1)S(1)} %fusion.54), kind=kOutput, calls=%fused_computation.54 | convolution fusion | flops 210241920 | bytes 8445952 | tf_op jit(solution)/shard_map/htu,uhd->thd/dot_general | solution.py:102
  285.2 5.1 %collective-permute-done.6 = f32[128,16,128]{0,2,1:T(8,128)} collective-permute-done((f32[128,16,128]{0,2,1:T(8,128)}, f32[128,16,128]{0,2,1:T(8,128)}, u32[]{:S(2)}, u32[]{:S(2)}) %collective-permute-start.6) | collective-permute-done | bytes 1048608 | tf_op jit(solution)/shard_map/ppermute | solution.py:14
  290.3 11.6 %collective-permute-done.5 = f32[128,16,128]{0,2,1:T(8,128)} collective-permute-done((f32[128,16,128]{0,2,1:T(8,128)}, f32[128,16,128]{0,2,1:T(8,128)}, u32[]{:S(2)}, u32[]{:S(2)}) %collective-permute-start.5) | collective-permute-done | bytes 1048608 | tf_op jit(solution)/shard_map/ppermute | solution.py:14
  304.9 105.0 %all-reduce.6.cloned.1.call-done = f32[128,128]{1,0:T(8,128)} async-done(((f32[128,128]{1,0:T(8,128)}), f32[128,128]{1,0:T(8,128)}) %all-reduce.6.cloned.1.call-update) | async-done | bytes 65552 | tf_op jit(solution)/shard_map/psum | solution.py:169
  (136 shorter events, 81.5 us)
Async XLA Ops:
  7.2 17.6 %copy-start.19 = (bf16[128,128]{1,0:T(8,128)(2,1)S(1)}, bf16[128,128]{1,0:T(8,128)(2,1)}, u32[]{:S(2)}) copy-start(bf16[128,128]{1,0:T(8,128)(2,1)} %param.14) | copy-start | bytes 98308
  7.2 17.9 %copy-start.16 = (bf16[128,2048]{1,0:T(8,128)(2,1)S(1)}, bf16[128,2048]{1,0:T(8,128)(2,1)}, u32[]{:S(2)}) copy-start(bf16[128,2048]{1,0:T(8,128)(2,1)} %param.11) | copy-start | bytes 1572868
  7.2 402.8 %all-reduce.6.cloned.1.call-start = ((), (), s32[]{:S(2)}) async-start(), calls=%async_computation | async-start | bytes 131072 | tf_op jit(solution)/shard_map/psum | solution.py:169
  8.6 17.4 %copy-start.17 = (bf16[128,2048]{1,0:T(8,128)(2,1)S(1)}, bf16[128,2048]{1,0:T(8,128)(2,1)}, u32[]{:S(2)}) copy-start(bf16[128,2048]{1,0:T(8,128)(2,1)} %param.18) | copy-start | bytes 1572868
  8.6 95.0 %collective-permute-start.4 = (bf16[128,2048]{0,1:T(8,128)(2,1)S(1)}, bf16[128,2048]{0,1:T(8,128)(2,1)}, u32[]{:S(2)}, u32[]{:S(2)}) collective-permute-start(bf16[128,2048]{0,1:T(8,128)(2,1)S(1)} %copy.70), channel_id=1, source_target_pairs={{0,4},{4,8},{8,12},{12,16},{16,20},{20,24},{24,28},{28,32},{32,36}... | collective-permute-start | bytes 1572872 | tf_op jit(solution)/shard_map/ppermute | solution.py:14
  13.7 90.0 %collective-permute-start.3 = (bf16[128,2048]{0,1:T(8,128)(2,1)S(1)}, bf16[128,2048]{0,1:T(8,128)(2,1)}, u32[]{:S(2)}, u32[]{:S(2)}) collective-permute-start(bf16[128,2048]{0,1:T(8,128)(2,1)S(1)} %copy.70), channel_id=1, source_target_pairs={{0,8},{4,12},{8,16},{12,20},{16,24},{20,28},{24,32},{28,36},{32,40... | collective-permute-start | bytes 1572872 | tf_op jit(solution)/shard_map/ppermute | solution.py:14
  19.3 9.1 %copy-start.8 = (bf16[128,2048]{0,1:T(8,128)(2,1)}, bf16[128,2048]{0,1:T(8,128)(2,1)S(1)}, u32[]{:S(2)}) copy-start(bf16[128,2048]{0,1:T(8,128)(2,1)S(1)} %copy.67) | copy-start | bytes 1572868
  19.4 7.7 %copy-start.21 = (s32[4]{0:T(128)S(1)}, s32[4]{0:T(128)}, u32[]{:S(2)}) copy-start(s32[4]{0:T(128)} %param.19) | copy-start | bytes 52
  19.4 8.0 %copy-start.18 = (bf16[128,2048]{1,0:T(8,128)(2,1)S(1)}, bf16[128,2048]{1,0:T(8,128)(2,1)}, u32[]{:S(2)}) copy-start(bf16[128,2048]{1,0:T(8,128)(2,1)} %param.16) | copy-start | bytes 1572868
  20.9 12.1 %copy-start.10 = (bf16[128,2048]{0,1:T(8,128)(2,1)}, bf16[128,2048]{0,1:T(8,128)(2,1)S(1)}, u32[]{:S(2)}) copy-start(bf16[128,2048]{0,1:T(8,128)(2,1)S(1)} %copy.66) | copy-start | bytes 1572868
  22.9 89.8 %collective-permute-start = (bf16[127,2048]{0,1:T(8,128)(2,1)}, bf16[127,2048]{0,1:T(8,128)(2,1)}, u32[]{:S(2)}, u32[]{:S(2)}) collective-permute-start(bf16[127,2048]{0,1:T(8,128)(2,1)} %slice.48), channel_id=1, source_target_pairs={{0,4},{4,8},{8,12},{12,16},{16,20},{20,24},{24,28},{28,32},{32,36}... | collective-permute-start | bytes 1560584 | tf_op jit(solution)/shard_map/ppermute | solution.py:14
  103.1 1.9 copy-start.15
  105.1 1.5 copy-start.4
  105.1 1.5 copy-start.12
  105.9 8.3 %slice-start = ((s8[8388608]{0:T(1024)(128)(4,1)}), s8[4194304]{0:T(1024)(128)(4,1)S(1)}, s32[]{:S(2)}) async-start(s8[8388608]{0:T(1024)(128)(4,1)} %bitcast.163), calls=%async_computation.1 | async-start | bytes 8388608
  106.6 7.6 %slice-start.1 = ((s8[8388608]{0:T(1024)(128)(4,1)}), s8[4194304]{0:T(1024)(128)(4,1)S(1)}, s32[]{:S(2)}) async-start(s8[8388608]{0:T(1024)(128)(4,1)} %bitcast.163), calls=%async_computation.2 | async-start | bytes 8388608
  107.4 5.2 %copy-start.7 = (bf16[128,2048]{0,1:T(8,128)(2,1)S(1)}, bf16[128,2048]{0,1:T(8,128)(2,1)}, u32[]{:S(2)}) copy-start(bf16[128,2048]{0,1:T(8,128)(2,1)} %copy-done.6) | copy-start | bytes 1572868
  107.7 25.6 %collective-permute-start.8 = (f32[128,16,128]{0,2,1:T(8,128)S(1)}, f32[128,16,128]{0,2,1:T(8,128)S(1)}, u32[]{:S(2)}, u32[]{:S(2)}) collective-permute-start(f32[128,16,128]{0,2,1:T(8,128)S(1)} %get-tuple-element.131), channel_id=1, source_target_pairs={{8,0},{12,4},{16,8},{20,12},{24,16},{28,20},{32,24},{36,28},{40,32... | collective-permute-start | bytes 3145736 | tf_op jit(solution)/shard_map/ppermute | solution.py:14
  109.3 36.7 %collective-permute-start.7 = (f32[128,16,128]{0,2,1:T(8,128)S(1)}, f32[128,16,128]{0,2,1:T(8,128)S(1)}, u32[]{:S(2)}, u32[]{:S(2)}) collective-permute-start(f32[128,16,128]{0,2,1:T(8,128)S(1)} %get-tuple-element.130), channel_id=1, source_target_pairs={{4,0},{8,4},{12,8},{16,12},{20,16},{24,20},{28,24},{32,28},{36,32}... | collective-permute-start | bytes 3145736 | tf_op jit(solution)/shard_map/ppermute | solution.py:14
  114.2 2.3 copy-start
  116.5 30.0 %copy-start.1 = (f32[128,16,128]{2,1,0:T(8,128)}, f32[128,16,128]{2,1,0:T(8,128)S(1)}, u32[]{:S(2)}) copy-start(f32[128,16,128]{2,1,0:T(8,128)S(1)} %fusion.10) | copy-start | bytes 3145732
  116.5 29.7 %copy-start.5 = (bf16[128,2048]{0,1:T(8,128)(2,1)S(1)}, bf16[128,2048]{0,1:T(8,128)(2,1)}, u32[]{:S(2)}) copy-start(bf16[128,2048]{0,1:T(8,128)(2,1)} %copy.65) | copy-start | bytes 1572868
  116.5 29.6 %copy-start.20 = (f32[2048]{0:T(1024)S(1)}, f32[2048]{0:T(1024)}, u32[]{:S(2)}) copy-start(f32[2048]{0:T(1024)} %param.15) | copy-start | bytes 24580
  159.2 88.9 %collective-permute-start.2 = (bf16[128,2048]{0,1:T(8,128)(2,1)}, bf16[128,2048]{0,1:T(8,128)(2,1)}, u32[]{:S(2)}, u32[]{:S(2)}) collective-permute-start(bf16[128,2048]{0,1:T(8,128)(2,1)} %get-tuple-element.134), channel_id=1, source_target_pairs={{0,4},{4,8},{8,12},{12,16},{16,20},{20,24},{24,28},{28,32},{32,36}... | collective-permute-start | bytes 1572872 | tf_op jit(solution)/shard_map/ppermute | solution.py:14
  163.0 85.1 %collective-permute-start.1 = (bf16[128,2048]{0,1:T(8,128)(2,1)}, bf16[128,2048]{0,1:T(8,128)(2,1)}, u32[]{:S(2)}, u32[]{:S(2)}) collective-permute-start(bf16[128,2048]{0,1:T(8,128)(2,1)} %get-tuple-element.134), channel_id=1, source_target_pairs={{0,8},{4,12},{8,16},{12,20},{16,24},{20,28},{24,32},{28,36},{32,40... | collective-permute-start | bytes 1572872 | tf_op jit(solution)/shard_map/ppermute | solution.py:14
  168.2 71.7 %collective-permute-start.9 = (bf16[127,2048]{0,1:T(8,128)(2,1)}, bf16[127,2048]{0,1:T(8,128)(2,1)}, u32[]{:S(2)}, u32[]{:S(2)}) collective-permute-start(bf16[127,2048]{0,1:T(8,128)(2,1)} %bitcast.150), channel_id=1, source_target_pairs={{4,0},{8,4},{12,8},{16,12},{20,16},{24,20},{28,24},{32,28},{36,32}... | collective-permute-start | bytes 1560584 | tf_op jit(solution)/shard_map/ppermute | solution.py:14
  248.1 2.8 copy-start.13
  259.8 6.8 %copy-start.9 = (bf16[128,2048]{0,1:T(8,128)(2,1)S(1)}, bf16[128,2048]{0,1:T(8,128)(2,1)}, u32[]{:S(2)}) copy-start(bf16[128,2048]{0,1:T(8,128)(2,1)} %copy-done.8) | copy-start | bytes 1572868
  259.8 6.8 %copy-start.11 = (bf16[128,2048]{0,1:T(8,128)(2,1)S(1)}, bf16[128,2048]{0,1:T(8,128)(2,1)}, u32[]{:S(2)}) copy-start(bf16[128,2048]{0,1:T(8,128)(2,1)} %copy-done.10) | copy-start | bytes 1572868
  259.8 6.8 %copy-start.14 = (f32[128,16,128]{2,1,0:T(8,128)S(1)}, f32[128,16,128]{2,1,0:T(8,128)}, u32[]{:S(2)}) copy-start(f32[128,16,128]{2,1,0:T(8,128)} %fusion.8) | copy-start | bytes 3145732
  263.2 27.1 %collective-permute-start.6 = (f32[128,16,128]{0,2,1:T(8,128)}, f32[128,16,128]{0,2,1:T(8,128)}, u32[]{:S(2)}, u32[]{:S(2)}) collective-permute-start(f32[128,16,128]{0,2,1:T(8,128)} %get-tuple-element.129), channel_id=1, source_target_pairs={{8,0},{12,4},{16,8},{20,12},{24,16},{28,20},{32,24},{36,28},{40,32... | collective-permute-start | bytes 3145736 | tf_op jit(solution)/shard_map/ppermute | solution.py:14
  264.5 37.4 %collective-permute-start.5 = (f32[128,16,128]{0,2,1:T(8,128)}, f32[128,16,128]{0,2,1:T(8,128)}, u32[]{:S(2)}, u32[]{:S(2)}) collective-permute-start(f32[128,16,128]{0,2,1:T(8,128)} %get-tuple-element.128), channel_id=1, source_target_pairs={{4,0},{8,4},{12,8},{16,12},{20,16},{24,20},{28,24},{32,28},{36,32}... | collective-permute-start | bytes 3145736 | tf_op jit(solution)/shard_map/ppermute | solution.py:14
  (3 other events, 2.9 us)
Sparse Core Ops, SparseCore 0:
  240.0 169.8 all-reduce.5
where the time goes:
time: 421 us; the launch traced here: 418 us
  local copies, waits for them, and re-layouts  155 us (37%)
  waiting for transfers between devices  151 us (36%)
  matrix products  35.9 us (9%)
  starting transfers between devices  30.6 us (7%)
  other arithmetic  21.9 us (5%)
  between operations  14.5 us (3%)
  blocking collectives  8.7 us (2%)
    psum x1, waiting for transfers between devices, body(): grad_filters = lax.psum(local_filters, ('context', 'mirror'))  105 us
    ppermute x10, waiting for transfers between devices, passed_along(): return lax.ppermute(block, axis, route)  46.1 us
    another operation x4, local copies, waits for them, and re-layouts, banded(): jnp.tile(band_table, (1, row_count + 1))[:, :row_count * col_count]  35.4 us
    reshape x4, local copies, waits for them, and re-layouts, filter_block(): flattened.reshape(block_size, tok_rows, pad_rows + 1)[:, :, :tap_count]  31.8 us
    ppermute x10, starting transfers between devices, passed_along(): return lax.ppermute(block, axis, route)  30.6 us
    reshape x2, local copies, waits for them, and re-layouts, banded(): return repeated.reshape(band_table.shape[0], row_count, col_count)  25 us
    unnamed x61, local copies, waits for them, and re-layouts  20.7 us
    slice x2, local copies, waits for them, and re-layouts, banded(): jnp.tile(band_table, (1, row_count + 1))[:, :row_count * col_count]  14.1 us
  transfers between devices with their start and end apart: 11, of which 5 were waited for; matrix products, arithmetic and copies ran while one was open for 49% of the time, Pallas kernels for 0%

commit v1 on v0

--- a/solution.py
+++ b/solution.py
@@ -166,7 +166,7 @@
         1, 0, 2, 3
     )
     local_filters = lax.map(filter_block, (grad_blocks, wide_blocks)).reshape(groups, tap_count)
-    grad_filters = lax.psum(local_filters, ("context", "mirror"))
+    grad_filters = jnp.sum(lax.all_gather(local_filters, ("context", "mirror")), axis=0)
     return (
         attn_out,
         grad_attn_q,

time: 421 us -> 330 us (0.78)
  the two profiles are of different devices: /device:TPU:1 before, /device:TPU:3 now
where the time goes in v1:
time: 330 us; the launch traced here: 327 us
  local copies, waits for them, and re-layouts  154 us (47%)
  waiting for transfers between devices  57.8 us (18%)
  matrix products  36 us (11%)
  starting transfers between devices  31 us (9%)
  other arithmetic  24.7 us (7%)
  between operations  14.6 us (4%)
  blocking collectives  8.88 us (3%)
    ppermute x10, waiting for transfers between devices, passed_along(): return lax.ppermute(block, axis, route)  57.7 us
    another operation x4, local copies, waits for them, and re-layouts, banded(): jnp.tile(band_table, (1, row_count + 1))[:, :row_count * col_count]  35.3 us
    reshape x4, local copies, waits for them, and re-layouts, filter_block(): flattened.reshape(block_size, tok_rows, pad_rows + 1)[:, :, :tap_count]  32 us
    ppermute x10, starting transfers between devices, passed_along(): return lax.ppermute(block, axis, route)  31 us
    reshape x2, local copies, waits for them, and re-layouts, banded(): return repeated.reshape(band_table.shape[0], row_count, col_count)  24.8 us
    unnamed x62, local copies, waits for them, and re-layouts  19.3 us
    slice x2, local copies, waits for them, and re-layouts, banded(): jnp.tile(band_table, (1, row_count + 1))[:, :row_count * col_count]  14.2 us
    while x4, local copies, waits for them, and re-layouts  9.72 us
  transfers between devices with their start and end apart: 11, of which 5 were waited for; matrix products, arithmetic and copies ran while one was open for 41% of the time, Pallas kernels for 0%

profile of v1, /device:TPU:3, one launch (start us, length us, event | category | flops | bytes accessed | tf_op | source)
XLA Modules:
  0.0 327.1 jit_solution(7787341624826637662)
XLA Ops:
  8.6 4.2 %collective-permute-start.4 = (bf16[128,2048]{0,1:T(8,128)(2,1)S(1)}, bf16[128,2048]{0,1:T(8,128)(2,1)}, u32[]{:S(2)}, u32[]{:S(2)}) collective-permute-start(bf16[128,2048]{0,1:T(8,128)(2,1)S(1)} %copy.96), channel_id=1, source_target_pairs={{0,4},{4,8},{8,12},{12,16},{16,20},{20,24},{24,28},{28,32},{32,36}... | collective-permute-start | bytes 1572872 | tf_op jit(solution)/shard_map/ppermute | solution.py:14
  12.8 3.5 %collective-permute-start.3 = (bf16[128,2048]{0,1:T(8,128)(2,1)S(1)}, bf16[128,2048]{0,1:T(8,128)(2,1)}, u32[]{:S(2)}, u32[]{:S(2)}) collective-permute-start(bf16[128,2048]{0,1:T(8,128)(2,1)S(1)} %copy.96), channel_id=1, source_target_pairs={{0,8},{4,12},{8,16},{12,20},{16,24},{20,28},{24,32},{28,36},{32,40... | collective-permute-start | bytes 1572872 | tf_op jit(solution)/shard_map/ppermute | solution.py:14
  27.1 4.4 %tile.8 = bf16[128,129,257]{0,2,1:T(8,128)(2,1)} broadcast(bf16[128,257]{0,1:T(8,128)(2,1)S(1)} %concatenate.19.clone), dimensions={0,2} | broadcast | bytes 8552960 | tf_op jit(solution)/shard_map/tile | solution.py:25
  31.5 13.2 %tile.9 = bf16[128,33153]{0,1:T(8,128)(2,1)} reshape(bf16[128,129,257]{0,2,1:T(8,128)(2,1)} %tile.8) | data formatting | bytes 16974336 | tf_op jit(solution)/shard_map/tile | solution.py:25
  44.7 7.1 %slice.49 = bf16[128,32768]{0,1:T(8,128)(2,1)} slice(bf16[128,33153]{0,1:T(8,128)(2,1)} %tile.9), slice={[0:128], [0:32768]} | slice | bytes 16777216 | tf_op jit(solution)/shard_map/slice | solution.py:25
  51.8 12.3 %copy.95 = bf16[128,128,256]{2,1,0:T(8,128)(2,1)} copy(bf16[128,128,256]{0,2,1:T(8,128)(2,1)} %bitcast.165) | data formatting | bytes 16777216 | tf_op jit(solution)/shard_map/reshape | solution.py:26
  68.7 4.1 %collective-permute-start.8 = (f32[128,16,128]{0,2,1:T(8,128)S(1)}, f32[128,16,128]{0,2,1:T(8,128)S(1)}, u32[]{:S(2)}, u32[]{:S(2)}) collective-permute-start(f32[128,16,128]{0,2,1:T(8,128)S(1)} %get-tuple-element.138), channel_id=1, source_target_pairs={{8,0},{12,4},{16,8},{20,12},{24,16},{28,20},{32,24},{36,28},{40,32... | collective-permute-start | bytes 3145736 | tf_op jit(solution)/shard_map/ppermute | solution.py:14
  79.1 16.6 %collective-permute-done.8 = f32[128,16,128]{0,2,1:T(8,128)S(1)} collective-permute-done((f32[128,16,128]{0,2,1:T(8,128)S(1)}, f32[128,16,128]{0,2,1:T(8,128)S(1)}, u32[]{:S(2)}, u32[]{:S(2)}) %collective-permute-start.8) | collective-permute-done | bytes 1048608 | tf_op jit(solution)/shard_map/ppermute | solution.py:14
  95.7 11.4 %collective-permute-done.7 = f32[128,16,128]{0,2,1:T(8,128)S(1)} collective-permute-done((f32[128,16,128]{0,2,1:T(8,128)S(1)}, f32[128,16,128]{0,2,1:T(8,128)S(1)}, u32[]{:S(2)}, u32[]{:S(2)}) %collective-permute-start.7) | collective-permute-done | bytes 1048608 | tf_op jit(solution)/shard_map/ppermute | solution.py:14
  108.3 8.9 %all-reduce.3 = (f32[128]{0:T(128)S(1)}, f32[128]{0:T(128)S(1)}) all-reduce(f32[128]{0:T(128)S(1)} %get-tuple-element.118, f32[128]{0:T(128)S(1)} %get-tuple-element.117), channel_id=1, replica_groups=mesh['context'=32,'mirror'=2,'tensor'=4] {'tensor'}, use_global_device_ids=true, to_apply=%region_4.5 | all-reduce | flops 256 | bytes 2048 | tf_op jit(solution)/shard_map/psum | solution.py:68
  117.2 3.4 %fusion.45 = (bf16[128,2048]{0,1:T(8,128)(2,1)}, bf16[128,2048]{0,1:T(8,128)(2,1)}, bf16[128,2048]{0,1:T(8,128)(2,1)}) fusion(bf16[128,2048]{0,1:T(8,128)(2,1)} %copy.91, f32[128]{0:T(128)S(1)} %get-tuple-element.146, f32[128,16,128]{2,1,0:T(8,128)} %copy-done.1, f32[128,16,128]{0,2,1:T(8,128)} %copy-done.2, f32[2048]{0:T(1024)S(1)} %copy-done.21, ...), kind=kLoop, calls=%fused_computation.55 | loop fusion | flops 3407872 | bytes 4203520 | tf_op jit(solution)/shard_map/convert_element_type | solution.py:129
  120.6 68.2 %while.13 = (s32[]{:T(128)}, f32[4,32,128]{2,1,0:T(8,128)}, bf16[4,128,32,16]{1,3,2,0:T(8,128)(2,1)}, bf16[4,256,32,16]{1,3,2,0:T(8,128)(2,1)}, s32[256]{0:T(256...) while((s32[]{:T(128)}, f32[4,32,128]{2,1,0:T(8,128)}, bf16[4,128,32,16]{1,3,2,0:T(8,128)(2,1)}, ...), condition=%wide.region_14.15_spmd.clone, body=%wide.region_12.14_spmd.clone.sunk | while | flops 35188736 | bytes 32246372 | solution.py:168
  127.2 8.0 %reshape.315 = f32[32,128,257]{2,1,0:T(8,128)} reshape(f32[32,32896]{1,0:T(8,128)} %pad.33) | data formatting | bytes 8421376 | tf_op jit(solution)/shard_map/while/body/eval_jaxpr/reshape | solution.py:159
  139.5 2.4 copy.129
  144.3 8.0 %reshape.315 = f32[32,128,257]{2,1,0:T(8,128)} reshape(f32[32,32896]{1,0:T(8,128)} %pad.33) | data formatting | bytes 8421376 | tf_op jit(solution)/shard_map/while/body/eval_jaxpr/reshape | solution.py:159
  161.4 8.0 %reshape.315 = f32[32,128,257]{2,1,0:T(8,128)} reshape(f32[32,32896]{1,0:T(8,128)} %pad.33) | data formatting | bytes 8421376 | tf_op jit(solution)/shard_map/while/body/eval_jaxpr/reshape | solution.py:159
  178.4 8.0 %reshape.315 = f32[32,128,257]{2,1,0:T(8,128)} reshape(f32[32,32896]{1,0:T(8,128)} %pad.33) | data formatting | bytes 8421376 | tf_op jit(solution)/shard_map/while/body/eval_jaxpr/reshape | solution.py:159
  188.8 4.2 %collective-permute-start.9 = (bf16[127,2048]{0,1:T(8,128)(2,1)}, bf16[127,2048]{0,1:T(8,128)(2,1)}, u32[]{:S(2)}, u32[]{:S(2)}) collective-permute-start(bf16[127,2048]{0,1:T(8,128)(2,1)} %bitcast.174), channel_id=1, source_target_pairs={{4,0},{8,4},{12,8},{16,12},{20,16},{24,20},{28,24},{32,28},{36,32}... | collective-permute-start | bytes 1560584 | tf_op jit(solution)/shard_map/ppermute | solution.py:14
  193.2 4.4 %tile.20 = bf16[128,129,257]{0,2,1:T(8,128)(2,1)} broadcast(bf16[128,257]{0,1:T(8,128)(2,1)S(1)} %concatenate.23.clone), dimensions={0,2} | broadcast | bytes 8552960 | tf_op jit(solution)/shard_map/tile | solution.py:25
  197.6 13.2 %tile.21 = bf16[128,33153]{0,1:T(8,128)(2,1)} reshape(bf16[128,129,257]{0,2,1:T(8,128)(2,1)} %tile.20) | data formatting | bytes 16974336 | tf_op jit(solution)/shard_map/tile | solution.py:25
  210.8 7.2 %slice.57 = bf16[128,32768]{0,1:T(8,128)(2,1)} slice(bf16[128,33153]{0,1:T(8,128)(2,1)} %tile.21), slice={[0:128], [0:32768]} | slice | bytes 16777216 | tf_op jit(solution)/shard_map/slice | solution.py:25
  218.0 12.5 %copy.110 = bf16[128,128,256]{2,1,0:T(8,128)(2,1)} copy(bf16[128,128,256]{0,2,1:T(8,128)(2,1)} %bitcast.166) | data formatting | bytes 16777216 | tf_op jit(solution)/shard_map/reshape | solution.py:26
  232.4 4.6 %collective-permute-start.1 = (bf16[128,2048]{0,1:T(8,128)(2,1)}, bf16[128,2048]{0,1:T(8,128)(2,1)}, u32[]{:S(2)}, u32[]{:S(2)}) collective-permute-start(bf16[128,2048]{0,1:T(8,128)(2,1)} %get-tuple-element.141), channel_id=1, source_target_pairs={{0,8},{4,12},{8,16},{12,20},{16,24},{20,28},{24,32},{28,36},{32,40... | collective-permute-start | bytes 1572872 | tf_op jit(solution)/shard_map/ppermute | solution.py:14
  240.5 6.7 %fusion.8 = f32[128,16,128]{2,1,0:T(8,128)} fusion(bf16[256,128,16]{0,2,1:T(8,128)(2,1)S(1)} %bitcast.178, bf16[128,128,256]{2,1,0:T(8,128)(2,1)} %copy.110, bf16[128,256]{1,0:T(8,128)(2,1)S(1)} %get-tuple-element.144), kind=kOutput, calls=%fused_computation.11 | convolution fusion | flops 138412032 | bytes 10551296 | tf_op jit(solution)/shard_map/gtu,ugc->tgc/dot_general | solution.py:138
  247.2 18.0 %collective-permute-done.1 = bf16[128,2048]{0,1:T(8,128)(2,1)} collective-permute-done((bf16[128,2048]{0,1:T(8,128)(2,1)}, bf16[128,2048]{0,1:T(8,128)(2,1)}, u32[]{:S(2)}, u32[]{:S(2)}) %collective-permute-start.1) | collective-permute-done | bytes 524320 | tf_op jit(solution)/shard_map/ppermute | solution.py:14
  270.2 6.7 %convolution_bitcast_fusion.1 = f32[384,16,128]{0,2,1:T(8,128)} fusion(bf16[128,16,128]{0,2,1:T(8,128)(2,1)} %bitcast.180, f32[16,384,128]{2,1,0:T(8,128)} %fusion.72, f32[16,384,128]{2,1,0:T(8,128)S(1)} %get-tuple-element.149, f32[16,128]{1,0:T(8,128)S(1)} %log_add_fusion, pred[128,384]{0,1:T(8,128)(4,1)S(1)} %fusion.54), kind=kOutput, calls=%fused_computation.32 | convolution fusion | flops 209979776 | bytes 10018816 | tf_op jit(solution)/shard_map/htu,thd->uhd/dot_general | solution.py:107
  276.9 3.2 fusion.70
  289.3 3.0 convolution_convert_fusion
  294.3 6.2 %fusion.44 = bf16[16,128,128]{2,1,0:T(8,128)(2,1)} fusion(bf16[384,16,128]{0,2,1:T(8,128)(2,1)} %bitcast.172, f32[16,384,128]{2,1,0:T(8,128)} %fusion.72, f32[16,384,128]{2,1,0:T(8,128)S(1)} %get-tuple-element.149, f32[16,128]{1,0:T(8,128)S(1)} %log_add_fusion, pred[128,384]{0,1:T(8,128)(4,1)S(1)} %fusion.54), kind=kOutput, calls=%fused_computation.54 | convolution fusion | flops 210241920 | bytes 8445952 | tf_op jit(solution)/shard_map/htu,uhd->thd/dot_general | solution.py:102
  302.5 4.7 %collective-permute-done.6 = f32[128,16,128]{0,2,1:T(8,128)} collective-permute-done((f32[128,16,128]{0,2,1:T(8,128)}, f32[128,16,128]{0,2,1:T(8,128)}, u32[]{:S(2)}, u32[]{:S(2)}) %collective-permute-start.6) | collective-permute-done | bytes 1048608 | tf_op jit(solution)/shard_map/ppermute | solution.py:14
  307.3 7.0 %collective-permute-done.5 = f32[128,16,128]{0,2,1:T(8,128)} collective-permute-done((f32[128,16,128]{0,2,1:T(8,128)}, f32[128,16,128]{0,2,1:T(8,128)}, u32[]{:S(2)}, u32[]{:S(2)}) %collective-permute-start.5) | collective-permute-done | bytes 1048608 | tf_op jit(solution)/shard_map/ppermute | solution.py:14
  317.3 3.0 reduce_sum.101
  (138 shorter events, 84.2 us)
Async XLA Ops:
  7.2 16.3 %copy-start.17 = (bf16[128,2048]{1,0:T(8,128)(2,1)S(1)}, bf16[128,2048]{1,0:T(8,128)(2,1)}, u32[]{:S(2)}) copy-start(bf16[128,2048]{1,0:T(8,128)(2,1)} %param.11) | copy-start | bytes 1572868
  7.2 310.1 %all-gather.2.cloned.1.call-start = ((), (), s32[]{:S(2)}) async-start(), calls=%async_computation | async-start | bytes 4259840 | tf_op jit(solution)/shard_map/all_gather | solution.py:169
  8.6 15.9 %copy-start.18 = (bf16[128,2048]{1,0:T(8,128)(2,1)S(1)}, bf16[128,2048]{1,0:T(8,128)(2,1)}, u32[]{:S(2)}) copy-start(bf16[128,2048]{1,0:T(8,128)(2,1)} %param.18) | copy-start | bytes 1572868
  8.6 56.0 %collective-permute-start.4 = (bf16[128,2048]{0,1:T(8,128)(2,1)S(1)}, bf16[128,2048]{0,1:T(8,128)(2,1)}, u32[]{:S(2)}, u32[]{:S(2)}) collective-permute-start(bf16[128,2048]{0,1:T(8,128)(2,1)S(1)} %copy.96), channel_id=1, source_target_pairs={{0,4},{4,8},{8,12},{12,16},{16,20},{20,24},{24,28},{28,32},{32,36}... | collective-permute-start | bytes 1572872 | tf_op jit(solution)/shard_map/ppermute | solution.py:14
  12.8 51.7 %collective-permute-start.3 = (bf16[128,2048]{0,1:T(8,128)(2,1)S(1)}, bf16[128,2048]{0,1:T(8,128)(2,1)}, u32[]{:S(2)}, u32[]{:S(2)}) collective-permute-start(bf16[128,2048]{0,1:T(8,128)(2,1)S(1)} %copy.96), channel_id=1, source_target_pairs={{0,8},{4,12},{8,16},{12,20},{16,24},{20,28},{24,32},{28,36},{32,40... | collective-permute-start | bytes 1572872 | tf_op jit(solution)/shard_map/ppermute | solution.py:14
  17.7 9.1 %copy-start.8 = (bf16[128,2048]{0,1:T(8,128)(2,1)}, bf16[128,2048]{0,1:T(8,128)(2,1)S(1)}, u32[]{:S(2)}) copy-start(bf16[128,2048]{0,1:T(8,128)(2,1)S(1)} %copy.93) | copy-start | bytes 1572868
  17.7 7.7 %copy-start.22 = (s32[4]{0:T(128)S(1)}, s32[4]{0:T(128)}, u32[]{:S(2)}) copy-start(s32[4]{0:T(128)} %param.19) | copy-start | bytes 52
  17.7 8.1 %copy-start.19 = (bf16[128,2048]{1,0:T(8,128)(2,1)S(1)}, bf16[128,2048]{1,0:T(8,128)(2,1)}, u32[]{:S(2)}) copy-start(bf16[128,2048]{1,0:T(8,128)(2,1)} %param.16) | copy-start | bytes 1572868
  19.3 12.3 %copy-start.10 = (bf16[128,2048]{0,1:T(8,128)(2,1)}, bf16[128,2048]{0,1:T(8,128)(2,1)S(1)}, u32[]{:S(2)}) copy-start(bf16[128,2048]{0,1:T(8,128)(2,1)S(1)} %copy.92) | copy-start | bytes 1572868
  19.3 7.6 %copy-start.20 = (bf16[128,128]{1,0:T(8,128)(2,1)S(1)}, bf16[128,128]{1,0:T(8,128)(2,1)}, u32[]{:S(2)}) copy-start(bf16[128,128]{1,0:T(8,128)(2,1)} %param.14) | copy-start | bytes 98308
  21.2 53.9 %collective-permute-start = (bf16[127,2048]{0,1:T(8,128)(2,1)}, bf16[127,2048]{0,1:T(8,128)(2,1)}, u32[]{:S(2)}, u32[]{:S(2)}) collective-permute-start(bf16[127,2048]{0,1:T(8,128)(2,1)} %slice.48), channel_id=1, source_target_pairs={{0,4},{4,8},{8,12},{12,16},{16,20},{20,24},{24,28},{28,32},{32,36}... | collective-permute-start | bytes 1560584 | tf_op jit(solution)/shard_map/ppermute | solution.py:14
  64.1 1.9 copy-start.16
  66.0 1.5 copy-start.12
  66.9 9.9 %slice-start = ((s8[8388608]{0:T(1024)(128)(4,1)}), s8[4194304]{0:T(1024)(128)(4,1)S(1)}, s32[]{:S(2)}) async-start(s8[8388608]{0:T(1024)(128)(4,1)} %bitcast.163), calls=%async_computation.1 | async-start | bytes 8388608
  67.6 9.2 %slice-start.1 = ((s8[8388608]{0:T(1024)(128)(4,1)}), s8[4194304]{0:T(1024)(128)(4,1)S(1)}, s32[]{:S(2)}) async-start(s8[8388608]{0:T(1024)(128)(4,1)} %bitcast.163), calls=%async_computation.2 | async-start | bytes 8388608
  68.4 6.8 %copy-start.7 = (bf16[128,2048]{0,1:T(8,128)(2,1)S(1)}, bf16[128,2048]{0,1:T(8,128)(2,1)}, u32[]{:S(2)}) copy-start(bf16[128,2048]{0,1:T(8,128)(2,1)} %copy-done.6) | copy-start | bytes 1572868
  68.7 27.0 %collective-permute-start.8 = (f32[128,16,128]{0,2,1:T(8,128)S(1)}, f32[128,16,128]{0,2,1:T(8,128)S(1)}, u32[]{:S(2)}, u32[]{:S(2)}) collective-permute-start(f32[128,16,128]{0,2,1:T(8,128)S(1)} %get-tuple-element.138), channel_id=1, source_target_pairs={{8,0},{12,4},{16,8},{20,12},{24,16},{28,20},{32,24},{36,28},{40,32... | collective-permute-start | bytes 3145736 | tf_op jit(solution)/shard_map/ppermute | solution.py:14
  72.8 34.3 %collective-permute-start.7 = (f32[128,16,128]{0,2,1:T(8,128)S(1)}, f32[128,16,128]{0,2,1:T(8,128)S(1)}, u32[]{:S(2)}, u32[]{:S(2)}) collective-permute-start(f32[128,16,128]{0,2,1:T(8,128)S(1)} %get-tuple-element.137), channel_id=1, source_target_pairs={{4,0},{8,4},{12,8},{16,12},{20,16},{24,20},{28,24},{32,28},{36,32}... | collective-permute-start | bytes 3145736 | tf_op jit(solution)/shard_map/ppermute | solution.py:14
  76.7 2.3 copy-start
  79.1 28.6 %copy-start.1 = (f32[128,16,128]{2,1,0:T(8,128)}, f32[128,16,128]{2,1,0:T(8,128)S(1)}, u32[]{:S(2)}) copy-start(f32[128,16,128]{2,1,0:T(8,128)S(1)} %fusion.10) | copy-start | bytes 3145732
  79.1 28.2 %copy-start.5 = (bf16[128,2048]{0,1:T(8,128)(2,1)S(1)}, bf16[128,2048]{0,1:T(8,128)(2,1)}, u32[]{:S(2)}) copy-start(bf16[128,2048]{0,1:T(8,128)(2,1)} %copy.91) | copy-start | bytes 1572868
  79.1 28.2 %copy-start.21 = (f32[2048]{0:T(1024)S(1)}, f32[2048]{0:T(1024)}, u32[]{:S(2)}) copy-start(f32[2048]{0:T(1024)} %param.15) | copy-start | bytes 24580
  188.8 50.2 %collective-permute-start.9 = (bf16[127,2048]{0,1:T(8,128)(2,1)}, bf16[127,2048]{0,1:T(8,128)(2,1)}, u32[]{:S(2)}, u32[]{:S(2)}) collective-permute-start(bf16[127,2048]{0,1:T(8,128)(2,1)} %bitcast.174), channel_id=1, source_target_pairs={{4,0},{8,4},{12,8},{16,12},{20,16},{24,20},{28,24},{32,28},{36,32}... | collective-permute-start | bytes 1560584 | tf_op jit(solution)/shard_map/ppermute | solution.py:14
  230.5 16.7 %collective-permute-start.2 = (bf16[128,2048]{0,1:T(8,128)(2,1)}, bf16[128,2048]{0,1:T(8,128)(2,1)}, u32[]{:S(2)}, u32[]{:S(2)}) collective-permute-start(bf16[128,2048]{0,1:T(8,128)(2,1)} %get-tuple-element.141), channel_id=1, source_target_pairs={{0,4},{4,8},{8,12},{12,16},{16,20},{20,24},{24,28},{28,32},{32,36}... | collective-permute-start | bytes 1572872 | tf_op jit(solution)/shard_map/ppermute | solution.py:14
  232.4 32.8 %collective-permute-start.1 = (bf16[128,2048]{0,1:T(8,128)(2,1)}, bf16[128,2048]{0,1:T(8,128)(2,1)}, u32[]{:S(2)}, u32[]{:S(2)}) collective-permute-start(bf16[128,2048]{0,1:T(8,128)(2,1)} %get-tuple-element.141), channel_id=1, source_target_pairs={{0,8},{4,12},{8,16},{12,20},{16,24},{20,28},{24,32},{28,36},{32,40... | collective-permute-start | bytes 1572872 | tf_op jit(solution)/shard_map/ppermute | solution.py:14
  240.5 24.8 %copy-start.15 = (bf16[128,2048]{0,1:T(8,128)(2,1)S(1)}, bf16[128,2048]{0,1:T(8,128)(2,1)}, u32[]{:S(2)}) copy-start(bf16[128,2048]{0,1:T(8,128)(2,1)} %get-tuple-element.141) | copy-start | bytes 1572868
  247.2 20.6 %copy-start.13 = (bf16[128,2048]{0,1:T(8,128)(2,1)S(1)}, bf16[128,2048]{0,1:T(8,128)(2,1)}, u32[]{:S(2)}) copy-start(bf16[128,2048]{0,1:T(8,128)(2,1)} %copy.126) | copy-start | bytes 1572868
  276.9 7.1 %copy-start.9 = (bf16[128,2048]{0,1:T(8,128)(2,1)S(1)}, bf16[128,2048]{0,1:T(8,128)(2,1)}, u32[]{:S(2)}) copy-start(bf16[128,2048]{0,1:T(8,128)(2,1)} %copy-done.8) | copy-start | bytes 1572868
  276.9 7.1 %copy-start.11 = (bf16[128,2048]{0,1:T(8,128)(2,1)S(1)}, bf16[128,2048]{0,1:T(8,128)(2,1)}, u32[]{:S(2)}) copy-start(bf16[128,2048]{0,1:T(8,128)(2,1)} %copy-done.10) | copy-start | bytes 1572868
  276.9 7.1 %copy-start.14 = (f32[128,16,128]{2,1,0:T(8,128)S(1)}, f32[128,16,128]{2,1,0:T(8,128)}, u32[]{:S(2)}) copy-start(f32[128,16,128]{2,1,0:T(8,128)} %fusion.8) | copy-start | bytes 3145732
  280.2 27.1 %collective-permute-start.6 = (f32[128,16,128]{0,2,1:T(8,128)}, f32[128,16,128]{0,2,1:T(8,128)}, u32[]{:S(2)}, u32[]{:S(2)}) collective-permute-start(f32[128,16,128]{0,2,1:T(8,128)} %get-tuple-element.136), channel_id=1, source_target_pairs={{8,0},{12,4},{16,8},{20,12},{24,16},{28,20},{32,24},{36,28},{40,32... | collective-permute-start | bytes 3145736 | tf_op jit(solution)/shard_map/ppermute | solution.py:14
  282.1 32.1 %collective-permute-start.5 = (f32[128,16,128]{0,2,1:T(8,128)}, f32[128,16,128]{0,2,1:T(8,128)}, u32[]{:S(2)}, u32[]{:S(2)}) collective-permute-start(f32[128,16,128]{0,2,1:T(8,128)} %get-tuple-element.135), channel_id=1, source_target_pairs={{4,0},{8,4},{12,8},{16,12},{20,16},{24,20},{28,24},{32,28},{36,32}... | collective-permute-start | bytes 3145736 | tf_op jit(solution)/shard_map/ppermute | solution.py:14
  (4 other events, 4.5 us)
Sparse Core Ops, SparseCore 0:
  189.0 80.4 all-gather.1
